TPU v7x, 32 devices: a whole 2x2x4 slice. The times are simulated.
32 devices in a mesh: rep: 8 (over z, core), shard: 4 (over y, x).
Axes of the slice: x: 2, y: 2, z: 4, core: 2. Of those that a mesh axis runs over, the one named last changes fastest.
Arguments:
- tokens: bfloat16 [32, 1024, 1024], P(('rep', 'shard')), may hold values from -6 to 6
- segments: int32 [32, 1024], P(('rep', 'shard')), may hold values from 0 to 7, never falling along the last dimension, each value on 1 to 512 neighbouring positions
- cotangent: bfloat16 [32, 1024, 1024], P(('rep', 'shard')), may hold values from -6 to 6
- norm_mix: bfloat16 [1024], P('shard'), may hold values from 0.5 to 1.5
- w_query: bfloat16 [1024, 512], P('shard'), may hold values from -0.1875 to 0.1875
- w_key: bfloat16 [1024, 512], P('shard'), may hold values from -0.1875 to 0.1875
- w_value: bfloat16 [1024, 1024], P('shard'), may hold values from -0.1875 to 0.1875
- w_outgate: bfloat16 [1024, 1024], P('shard'), may hold values from -0.1875 to 0.1875
- w_low: bfloat16 [1024, 16], P('shard'), may hold values from -0.1875 to 0.1875
- w_high: bfloat16 [16, 512], P(None, 'shard'), may hold values from -1.5 to 1.5
- decay_bias: bfloat16 [512], P('shard'), may hold values from 0.5 to 4.5
- head_gain: bfloat16 [256], P('shard'), may hold values from 0.5 to 1.5
- w_out: bfloat16 [1024, 1024], P('shard'), may hold values from -0.1875 to 0.1875
- norm_mlp: bfloat16 [1024], P('shard'), may hold values from 0.5 to 1.5
- w_gate: bfloat16 [1024, 2816], P('shard'), may hold values from -0.1875 to 0.1875
- w_up: bfloat16 [1024, 2816], P('shard'), may hold values from -0.1875 to 0.1875
- w_down: bfloat16 [2816, 1024], P('shard'), may hold values from -0.109375 to 0.109375
Outputs:
- block_out: bfloat16 [32, 1024, 1024], P(('rep', 'shard'))
- grad_tokens: float32 [32, 1024, 1024], P(('rep', 'shard'))
- grad_norm_mix: float32 [1024], P('shard')
- grad_w_query: float32 [1024, 512], P('shard')
- grad_w_key: float32 [1024, 512], P('shard')
- grad_w_value: float32 [1024, 1024], P('shard')
- grad_w_outgate: float32 [1024, 1024], P('shard')
- grad_w_low: float32 [1024, 16], P('shard')
- grad_w_high: float32 [16, 512], P(None, 'shard')
- grad_decay_bias: float32 [512], P('shard')
- grad_head_gain: float32 [256], P('shard')
- grad_w_out: float32 [1024, 1024], P('shard')
- grad_norm_mlp: float32 [1024], P('shard')
- grad_w_gate: float32 [1024, 2816], P('shard')
- grad_w_up: float32 [1024, 2816], P('shard')
- grad_w_down: float32 [2816, 1024], P('shard')
Inputs may be any that keep to these rules, and one draw needn't show every extreme that they name: `segments`: segment numbers never fall along a sequence; a document has 1 to 512 tokens and some document has exactly 512.
All inputs are finite; a program needn't handle non-finite values.
Results may differ from a plain program's by a relative error of at most 0.018.
Values may be sent and summed in bfloat16 or wider, within the bound.
A program may use at most 256 MiB of HBM per device.

v0:
```python
from functools import partial
import jax
import jax.numpy as jnp
from jax import lax
from jax.sharding import PartitionSpec as P

HEADS = 4
KH = 128
VH = 256
BLOCK = 64
VD = 1024
HEAD_EPS = 1.0


def matmul(left, right):
    return jnp.dot(left, right, preferred_element_type=jnp.float32)


def left_trans(left, right):
    return lax.dot_general(
        left, right, (((0,), (0,)), ((), ())), preferred_element_type=jnp.float32
    )


def right_trans(left, right):
    return lax.dot_general(
        left, right, (((1,), (1,)), ((), ())), preferred_element_type=jnp.float32
    )


def rms_scale(values, gain, epsilon=1e-05):
    inverse = lax.rsqrt(jnp.mean(values * values, axis=-1, keepdims=True) + epsilon)
    return values * inverse * gain


def block_pass(query, keys, values, decay, segment):
    length, heads, key_size = query.shape
    value_size = values.shape[-1]
    blocks = length // BLOCK
    query = query * key_size ** (-0.5)
    lower = lax.broadcasted_iota(jnp.int32, (BLOCK, BLOCK), 0) >= lax.broadcasted_iota(
        jnp.int32, (BLOCK, BLOCK), 1
    )

    def advance(carry, item):
        state, last_seg = carry
        qblk, kblk, vblk, dblk, sblk = item
        cumul = jnp.cumsum(dblk, axis=0)
        q_scaled = qblk * jnp.exp(cumul)
        k_scaled = kblk * jnp.exp(-cumul)
        same = ((sblk[:, None] == sblk[None, :]) & lower).astype(jnp.float32)
        scores = (
            jnp.einsum("thd,shd->hts", q_scaled, k_scaled, precision=lax.Precision.HIGHEST)
            * same[None]
        )
        inner = jnp.einsum("hts,she->the", scores, vblk, precision=lax.Precision.HIGHEST)
        keep = (sblk == last_seg).astype(jnp.float32)
        carried = (
            jnp.einsum("thd,hde->the", q_scaled, state, precision=lax.Precision.HIGHEST)
            * keep[:, None, None]
        )
        final = cumul[-1]
        tail = (sblk == sblk[-1]).astype(jnp.float32)
        scaled = k_scaled * jnp.exp(final)[None] * tail[:, None, None]
        fresh = jnp.einsum("shd,she->hde", scaled, vblk, precision=lax.Precision.HIGHEST)
        stay = (sblk[-1] == last_seg).astype(jnp.float32)
        state = jnp.exp(final)[:, :, None] * state * stay + fresh
        return ((state, sblk[-1]), inner + carried)

    def shaped(array):
        return array.reshape((blocks, BLOCK) + array.shape[1:])

    start = (jnp.zeros((heads, key_size, value_size), jnp.float32), jnp.int32(-1))
    _, outputs = lax.scan(
        jax.checkpoint(advance),
        start,
        (shaped(query), shaped(keys), shaped(values), shaped(decay), shaped(segment)),
    )
    return outputs.reshape(length, heads, value_size)


def mixer_core(query, keys, values, outgate, lowpre, decay_bias, head_gain, segment):
    total = query.shape[0]
    seqs = segment.shape[0]
    length = segment.shape[1]
    decay = jax.nn.log_sigmoid(lowpre + decay_bias) / 16.0

    def split(array, width):
        return array.reshape(seqs, length, HEADS, width)

    mixed = jax.vmap(block_pass)(
        split(query, KH), split(keys, KH), split(values, VH), split(decay, KH), segment
    )
    normed = rms_scale(mixed, head_gain, HEAD_EPS)
    return normed.reshape(total, VD) * jax.nn.silu(outgate)


def local(
    tokens,
    segments,
    cotangent,
    norm_mix,
    w_query,
    w_key,
    w_value,
    w_outgate,
    w_low,
    w_high,
    decay_bias,
    head_gain,
    w_out,
    norm_mlp,
    w_gate,
    w_up,
    w_down,
):
    mixer_full = (
        lax.all_gather(norm_mix, "shard", axis=0, tiled=True),
        lax.all_gather(w_query, "shard", axis=0, tiled=True),
        lax.all_gather(w_key, "shard", axis=0, tiled=True),
        lax.all_gather(w_value, "shard", axis=0, tiled=True),
        lax.all_gather(w_outgate, "shard", axis=0, tiled=True),
        lax.all_gather(w_low, "shard", axis=0, tiled=True),
        lax.all_gather(w_high, "shard", axis=1, tiled=True),
        lax.all_gather(decay_bias, "shard", axis=0, tiled=True),
        lax.all_gather(head_gain, "shard", axis=0, tiled=True),
        lax.all_gather(w_out, "shard", axis=0, tiled=True),
    )
    feed_full = (
        lax.all_gather(norm_mlp, "shard", axis=0, tiled=True),
        lax.all_gather(w_gate, "shard", axis=0, tiled=True),
        lax.all_gather(w_up, "shard", axis=0, tiled=True),
        lax.all_gather(w_down, "shard", axis=0, tiled=True),
    )
    gain_mix, query_w, key_w, value_w, outgate_w, low_w, high_w, bias_w, headgain_w, out_w = (
        mixer_full
    )
    gain_feed, gate_w, up_w, down_w = feed_full
    total = tokens.shape[0] * tokens.shape[1]
    width = tokens.shape[2]
    inputs = tokens.reshape(total, width).astype(jnp.float32)
    normed_mix, mix_pull = jax.vjp(rms_scale, inputs, gain_mix.astype(jnp.float32))
    first = normed_mix.astype(jnp.bfloat16)
    query = matmul(first, query_w)
    keys = matmul(first, key_w)
    values = matmul(first, value_w)
    outgate = matmul(first, outgate_w)
    lowrank = matmul(first, low_w).astype(jnp.bfloat16)
    lowpre = matmul(lowrank, high_w)
    core_local = partial(mixer_core, segment=segments)
    mixed, core_pull = jax.vjp(
        core_local,
        query,
        keys,
        values,
        outgate,
        lowpre,
        bias_w.astype(jnp.float32),
        headgain_w.astype(jnp.float32),
    )
    mixed_low = mixed.astype(jnp.bfloat16)
    resid = inputs + matmul(mixed_low, out_w)
    normed_feed, feed_pull = jax.vjp(rms_scale, resid, gain_feed.astype(jnp.float32))
    second = normed_feed.astype(jnp.bfloat16)
    gate = matmul(second, gate_w)
    upward = matmul(second, up_w)
    sigma = jax.nn.sigmoid(gate)
    swish = gate * sigma
    hidden = (swish * upward).astype(jnp.bfloat16)
    result = (resid + matmul(hidden, down_w)).astype(jnp.bfloat16)
    feed_back = (
        lax.all_gather(norm_mlp, "shard", axis=0, tiled=True),
        lax.all_gather(w_gate, "shard", axis=0, tiled=True),
        lax.all_gather(w_up, "shard", axis=0, tiled=True),
        lax.all_gather(w_down, "shard", axis=0, tiled=True),
    )
    unused_gain, back_gate, back_up, back_down = feed_back
    grad_out = cotangent.reshape(total, width)
    part_down = left_trans(hidden, grad_out)
    grad_hidden = right_trans(grad_out, back_down)
    slope = sigma * (1.0 + gate * (1.0 - sigma))
    grad_gate = (grad_hidden * upward * slope).astype(jnp.bfloat16)
    grad_up = (grad_hidden * swish).astype(jnp.bfloat16)
    part_gate = left_trans(second, grad_gate)
    part_up = left_trans(second, grad_up)
    grad_second = right_trans(grad_gate, back_gate) + right_trans(grad_up, back_up)
    grad_resid_norm, part_norm_mlp = feed_pull(grad_second)
    grad_resid = grad_out.astype(jnp.float32) + grad_resid_norm
    grad_branch = grad_resid.astype(jnp.bfloat16)
    mixer_back = (
        lax.all_gather(norm_mix, "shard", axis=0, tiled=True),
        lax.all_gather(w_query, "shard", axis=0, tiled=True),
        lax.all_gather(w_key, "shard", axis=0, tiled=True),
        lax.all_gather(w_value, "shard", axis=0, tiled=True),
        lax.all_gather(w_outgate, "shard", axis=0, tiled=True),
        lax.all_gather(w_low, "shard", axis=0, tiled=True),
        lax.all_gather(w_high, "shard", axis=1, tiled=True),
        lax.all_gather(decay_bias, "shard", axis=0, tiled=True),
        lax.all_gather(head_gain, "shard", axis=0, tiled=True),
        lax.all_gather(w_out, "shard", axis=0, tiled=True),
    )
    (
        unused_mix,
        back_query,
        back_key,
        back_value,
        back_outgate,
        back_low,
        back_high,
        unused_bias,
        unused_headgain,
        back_out,
    ) = mixer_back
    part_out = left_trans(mixed_low, grad_branch)
    grad_mixed = right_trans(grad_branch, back_out)
    grad_query, grad_keys, grad_values, grad_outgate, grad_lowpre, part_bias, part_headgain = (
        core_pull(grad_mixed)
    )
    grad_query = grad_query.astype(jnp.bfloat16)
    grad_keys = grad_keys.astype(jnp.bfloat16)
    grad_values = grad_values.astype(jnp.bfloat16)
    grad_outgate = grad_outgate.astype(jnp.bfloat16)
    grad_lowpre = grad_lowpre.astype(jnp.bfloat16)
    part_high = left_trans(lowrank, grad_lowpre)
    grad_lowrank = right_trans(grad_lowpre, back_high).astype(jnp.bfloat16)
    part_low = left_trans(first, grad_lowrank)
    part_query = left_trans(first, grad_query)
    part_key = left_trans(first, grad_keys)
    part_value = left_trans(first, grad_values)
    part_outgate = left_trans(first, grad_outgate)
    grad_first = (
        right_trans(grad_query, back_query)
        + right_trans(grad_keys, back_key)
        + right_trans(grad_values, back_value)
    )
    grad_first = (
        grad_first + right_trans(grad_outgate, back_outgate) + right_trans(grad_lowrank, back_low)
    )
    grad_inputs_norm, part_norm_mix = mix_pull(grad_first)
    grad_inputs = (grad_resid + grad_inputs_norm).reshape(tokens.shape)
    feed_rows = (
        lax.psum_scatter(
            part_norm_mlp.astype(jnp.bfloat16), "shard", scatter_dimension=0, tiled=True
        ).astype(jnp.float32),
        lax.psum_scatter(
            part_gate.astype(jnp.bfloat16), "shard", scatter_dimension=0, tiled=True
        ).astype(jnp.float32),
        lax.psum_scatter(
            part_up.astype(jnp.bfloat16), "shard", scatter_dimension=0, tiled=True
        ).astype(jnp.float32),
        lax.psum_scatter(
            part_down.astype(jnp.bfloat16), "shard", scatter_dimension=0, tiled=True
        ).astype(jnp.float32),
    )
    feed_sums = (
        lax.psum(feed_rows[0].astype(jnp.bfloat16), "rep").astype(jnp.float32),
        lax.psum(feed_rows[1].astype(jnp.bfloat16), "rep").astype(jnp.float32),
        lax.psum(feed_rows[2].astype(jnp.bfloat16), "rep").astype(jnp.float32),
        lax.psum(feed_rows[3].astype(jnp.bfloat16), "rep").astype(jnp.float32),
    )
    mixer_rows = (
        lax.psum_scatter(
            part_norm_mix.astype(jnp.bfloat16), "shard", scatter_dimension=0, tiled=True
        ).astype(jnp.float32),
        lax.psum_scatter(
            part_query.astype(jnp.bfloat16), "shard", scatter_dimension=0, tiled=True
        ).astype(jnp.float32),
        lax.psum_scatter(
            part_key.astype(jnp.bfloat16), "shard", scatter_dimension=0, tiled=True
        ).astype(jnp.float32),
        lax.psum_scatter(
            part_value.astype(jnp.bfloat16), "shard", scatter_dimension=0, tiled=True
        ).astype(jnp.float32),
        lax.psum_scatter(
            part_outgate.astype(jnp.bfloat16), "shard", scatter_dimension=0, tiled=True
        ).astype(jnp.float32),
        lax.psum_scatter(
            part_low.astype(jnp.bfloat16), "shard", scatter_dimension=0, tiled=True
        ).astype(jnp.float32),
        lax.psum_scatter(
            part_high.astype(jnp.bfloat16), "shard", scatter_dimension=1, tiled=True
        ).astype(jnp.float32),
        lax.psum_scatter(
            part_bias.astype(jnp.bfloat16), "shard", scatter_dimension=0, tiled=True
        ).astype(jnp.float32),
        lax.psum_scatter(
            part_headgain.astype(jnp.bfloat16), "shard", scatter_dimension=0, tiled=True
        ).astype(jnp.float32),
        lax.psum_scatter(
            part_out.astype(jnp.bfloat16), "shard", scatter_dimension=0, tiled=True
        ).astype(jnp.float32),
    )
    mixer_sums = (
        lax.psum(mixer_rows[0].astype(jnp.bfloat16), "rep").astype(jnp.float32),
        lax.psum(mixer_rows[1].astype(jnp.bfloat16), "rep").astype(jnp.float32),
        lax.psum(mixer_rows[2].astype(jnp.bfloat16), "rep").astype(jnp.float32),
        lax.psum(mixer_rows[3].astype(jnp.bfloat16), "rep").astype(jnp.float32),
        lax.psum(mixer_rows[4].astype(jnp.bfloat16), "rep").astype(jnp.float32),
        lax.psum(mixer_rows[5].astype(jnp.bfloat16), "rep").astype(jnp.float32),
        lax.psum(mixer_rows[6].astype(jnp.bfloat16), "rep").astype(jnp.float32),
        lax.psum(mixer_rows[7].astype(jnp.bfloat16), "rep").astype(jnp.float32),
        lax.psum(mixer_rows[8].astype(jnp.bfloat16), "rep").astype(jnp.float32),
        lax.psum(mixer_rows[9].astype(jnp.bfloat16), "rep").astype(jnp.float32),
    )
    return (
        result.reshape(tokens.shape),
        grad_inputs,
        mixer_sums[0],
        mixer_sums[1],
        mixer_sums[2],
        mixer_sums[3],
        mixer_sums[4],
        mixer_sums[5],
        mixer_sums[6],
        mixer_sums[7],
        mixer_sums[8],
        mixer_sums[9],
        feed_sums[0],
        feed_sums[1],
        feed_sums[2],
        feed_sums[3],
    )


def solution(mesh):
    in_specs = (
        P(("rep", "shard"), None, None),
        P(("rep", "shard"), None),
        P(("rep", "shard"), None, None),
        P("shard"),
        P("shard", None),
        P("shard", None),
        P("shard", None),
        P("shard", None),
        P("shard", None),
        P(None, "shard"),
        P("shard"),
        P("shard"),
        P("shard", None),
        P("shard"),
        P("shard", None),
        P("shard", None),
        P("shard", None),
    )
    out_specs = (
        P(("rep", "shard"), None, None),
        P(("rep", "shard"), None, None),
        P("shard"),
        P("shard", None),
        P("shard", None),
        P("shard", None),
        P("shard", None),
        P("shard", None),
        P(None, "shard"),
        P("shard"),
        P("shard"),
        P("shard", None),
        P("shard"),
        P("shard", None),
        P("shard", None),
        P("shard", None),
    )
    return jax.shard_map(local, mesh=mesh, in_specs=in_specs, out_specs=out_specs, check_vma=False)
```

profile of v0, /device:TPU:0, one launch (start us, length us, event | category | flops | bytes accessed | tf_op | source)
XLA Modules:
  0.0 1311.7 jit_solution(10404058792352158195)
XLA Ops:
  15.6 2.9 copy.180
  19.0 9.5 all-gather
  30.4 4.1 copy.181
  34.5 8.0 all_gather.53
  43.2 7.2 all_gather.54
  50.4 7.7 all-gather.1
  58.2 3.4 negate_multiply_fusion
  61.6 2.9 reshape.789
  67.3 8.9 all-reduce.1
  76.8 7.2 all-gather.2
  84.0 4.1 copy.194
  88.1 2.3 copy.182
  90.4 2.3 copy.184
  92.7 4.6 fusion.120
  97.3 2.6 fusion.158
  99.9 5.3 all-gather.14.cloned.1.call-done
  105.2 4.0 copy.183
  109.2 6.5 convolution_bitcast_fusion.6
  115.7 177.9 %while.44 = (s32[]{:T(128)}, f32[1,4,128,256]{3,2,1,0:T(8,128)S(1)}, s32[1]{0:T(128)}, f32[16,1,64,4,256]{4,2,3,1,0:T(8,128)}, f32[16,1,4,128,256]{4,3,2,1,0:T(8...) while((s32[]{:T(128)}, ...), condition=%wide.region_3.4_spmd.clone.clone, body=%wide.region_1.3_spmd.clone.sunk.clone | while | flops 280002816 | bytes 6207163 | solution.py:74
  293.6 7.1 copy.190
  303.2 3.0 copy.250
  306.2 3.0 copy.249
  309.2 8.6 multiply_convert_fusion.4
  317.8 4.8 multiply_reduce_fusion.6
  326.5 11.6 fusion.159
  338.1 12.9 fusion.160
  351.0 31.2 %all-gather.26.cloned.1.call-done = bf16[2816,1024]{1,0:T(8,128)(2,1)} async-done(((bf16[704,1024]{1,0:T(8,128)(2,1)}), bf16[2816,1024]{1,0:T(8,128)(2,1)}) %all-gather.26.cloned.1.call-update) | async-done | bytes 5767184 | tf_op jit(solution)/shard_map/all_gather | solution.py:133
  382.2 21.6 %multiply_convert_fusion = (bf16[1024,2816]{1,0:T(8,128)(2,1)}, bf16[1024,2816]{1,0:T(8,128)(2,1)}, bf16[1024,2816]{1,0:T(8,128)(2,1)}) fusion(f32[1024,2816]{1,0:T(8,128)} %fusion.159, f32[1024,2816]{1,0:T(8,128)} %fusion.160, bf16[2816,1024]{1,0:T(8,128)(2,1)} %all-gather.26.cloned.1.call-done, bf16[1,1024,1024]{2,1,0:T(8,128)(2,1)S(1)} %copy-done.19), kind=kOutput, calls=%fused_computation.120 | convolution fusion | flops 5948833792 | bytes 48234496 | tf_op jit(solution)/shard_map/dot_general | solution.py:26
  403.8 10.2 fusion.161
  414.1 6.5 multiply_reduce_fusion.2
  422.2 2.7 copy-done.60
  426.1 6.0 multiply_reduce_fusion.3
  432.2 5.7 reshape.794
  437.9 4.4 multiply_reduce_fusion.4
  443.8 2.6 add_add_fusion.1
  449.8 259.2 %while.45 = (s32[]{:T(128)}, f32[1,4,128,256]{2,3,1,0:T(8,128)S(1)}, f32[16,1,64,4,128]{4,2,3,1,0:T(8,128)}, bf16[16,1,64,4,128]{4,2,3,1,0:T(8,128)(2,1)}, bf16[...) while((s32[]{:T(128)}, ...), condition=%wide.region_13.14_spmd.clone.clone, body=%wide.region_8.13_spmd.clone.sunk.clone | while | flops 585089280 | bytes 16077553 | solution.py:74
  719.7 6.8 convolution_convert_fusion.3
  730.7 3.7 fusion.117
  734.5 5.3 convolution_convert_fusion.4
  739.9 10.9 convolution_convert_fusion.2
  750.9 11.1 convolution_convert_fusion.1
  762.3 11.1 convolution_convert_fusion
  775.4 2.3 multiply_negate_fusion
  781.9 2.3 convolution_convert_fusion.7
  785.9 6.7 fusion.162
  792.6 3.3 fusion.133
  795.9 4.4 fusion.163
  800.3 3.3 fusion.130
  803.7 8.0 reduce-scatter.23.cloned.1.call-done
  811.7 38.9 %reduce-scatter.17.cloned.1.call-done = bf16[256,1024]{1,0:T(8,128)(2,1)} async-done(((bf16[1024,1024]{1,0:T(8,128)(2,1)}), bf16[256,1024]{1,0:T(8,128)(2,1)}) %reduce-scatter.17.cloned.1.call-update) | async-done | bytes 524304 | tf_op jit(solution)/shard_map/reduce_scatter | solution.py:271
  850.6 38.2 %reduce-scatter.19.cloned.1.call-done = bf16[256,1024]{1,0:T(8,128)(2,1)} async-done(((bf16[1024,1024]{1,0:T(8,128)(2,1)}), bf16[256,1024]{1,0:T(8,128)(2,1)}) %reduce-scatter.19.cloned.1.call-update) | async-done | bytes 524304 | tf_op jit(solution)/shard_map/reduce_scatter | solution.py:274
  888.8 69.0 %reduce-scatter.25.cloned.1.call-done = bf16[256,2816]{1,0:T(8,128)(2,1)} async-done(((bf16[1024,2816]{1,0:T(8,128)(2,1)}), bf16[256,2816]{1,0:T(8,128)(2,1)}) %reduce-scatter.25.cloned.1.call-update) | async-done | bytes 1441808 | tf_op jit(solution)/shard_map/reduce_scatter | solution.py:245
  957.8 68.9 %reduce-scatter.27.cloned.1.call-done = bf16[256,2816]{1,0:T(8,128)(2,1)} async-done(((bf16[1024,2816]{1,0:T(8,128)(2,1)}), bf16[256,2816]{1,0:T(8,128)(2,1)}) %reduce-scatter.27.cloned.1.call-update) | async-done | bytes 1441808 | tf_op jit(solution)/shard_map/reduce_scatter | solution.py:248
  1026.7 68.9 %reduce-scatter.29.cloned.1.call-done = bf16[704,1024]{1,0:T(8,128)(2,1)} async-done(((bf16[2816,1024]{1,0:T(8,128)(2,1)}), bf16[704,1024]{1,0:T(8,128)(2,1)}) %reduce-scatter.29.cloned.1.call-update) | async-done | bytes 1441808 | tf_op jit(solution)/shard_map/reduce_scatter | solution.py:251
  1095.7 8.9 fusion.90
  1104.6 9.4 all-reduce.8
  1114.2 6.4 fusion.100
  1120.6 5.4 copy.213
  1126.0 10.6 fusion.102
  1136.5 2.6 copy.212
  1140.1 8.4 reduce-scatter.21.cloned.1.call-done
  1148.5 29.1 %all-reduce.6 = (bf16[256]{0:T(256)(128)(2,1)S(1)}, bf16[256,16]{0,1:T(8,128)(2,1)S(1)}, bf16[16,128]{1,0:T(8,128)(2,1)S(1)}, bf16[128]{0:T(256)(128)(2,1)S(1)},...) all-reduce(bf16[256]{0:T(256)(128)(2,1)S(1)} %dynamic-slice.2, ...), channel_id=1, replica_groups=mesh['rep'=8,'shard'=4] {'rep'}, use_global_device_ids=true, to_apply=%region_17.18 | all-reduce | flops 6848 | bytes 27392 | tf_op jit(solution)/shard_map/psum | solution.py:294
  1181.0 112.0 %all-reduce.11.cloned.1.call-done = (bf16[256,512]{1,0:T(8,128)(2,1)}, bf16[256,512]{1,0:T(8,128)(2,1)}, bf16[256,1024]{1,0:T(8,128)(2,1)}, bf16[256,1024]{1,0:T...) async-done(((bf16[256,512]{1,0:T(8,128)(2,1)}, bf16[256,512]{1,0:T(8,128)(2,1)}, ...) | async-done | bytes 6422544 | tf_op jit(solution)/shard_map/psum | solution.py:295
  1293.0 3.3 convert_element_type.335
  (961 shorter events, 455.0 us)
Async XLA Ops:
  7.2 81.0 %all-gather.12.cloned.1.call-start = ((), (), s32[]{:S(2)}) async-start(), calls=%async_computation.10 | async-start | bytes 1310720 | tf_op jit(solution)/shard_map/all_gather | solution.py:120
  7.9 82.5 %all-gather.16.cloned.1.call-start = ((), (), s32[]{:S(2)}) async-start(), calls=%async_computation.12 | async-start | bytes 1310720 | tf_op jit(solution)/shard_map/all_gather | solution.py:119
  8.7 96.6 %all-gather.14.cloned.1.call-start = ((), (), s32[]{:S(2)}) async-start(), calls=%async_computation.11 | async-start | bytes 2621440 | tf_op jit(solution)/shard_map/all_gather | solution.py:121
  9.4 299.8 %all-gather.18.cloned.1.call-start = ((), (), s32[]{:S(2)}) async-start(), calls=%async_computation.13 | async-start | bytes 2621440 | tf_op jit(solution)/shard_map/all_gather | solution.py:122
  10.0 307.8 %all-gather.20.cloned.1.call-start = ((), (), s32[]{:S(2)}) async-start(), calls=%async_computation.14 | async-start | bytes 2621440 | tf_op jit(solution)/shard_map/all_gather | solution.py:127
  10.6 314.6 %all-gather.22.cloned.1.call-start = ((), (), s32[]{:S(2)}) async-start(), calls=%async_computation.15 | async-start | bytes 7208960 | tf_op jit(solution)/shard_map/all_gather | solution.py:131
  11.1 327.0 %all-gather.24.cloned.1.call-start = ((), (), s32[]{:S(2)}) async-start(), calls=%async_computation.16 | async-start | bytes 7208960 | tf_op jit(solution)/shard_map/all_gather | solution.py:132
  11.9 370.3 %all-gather.26.cloned.1.call-start = ((), (), s32[]{:S(2)}) async-start(), calls=%async_computation.17 | async-start | bytes 7208960 | tf_op jit(solution)/shard_map/all_gather | solution.py:133
  12.6 791.0 %reduce-scatter.13.cloned.1.call-start = ((), (), s32[]{:S(2)}) async-start(), calls=%async_computation.18 | async-start | bytes 1310720 | tf_op jit(solution)/shard_map/reduce_scatter | solution.py:265
  14.4 4.6 copy-start.56
  18.4 299.3 %copy-start.2 = (bf16[1,1024,1024]{1,2,0:T(8,128)(2,1)}, bf16[1,1024,1024]{1,2,0:T(8,128)(2,1)S(1)}, u32[]{:S(2)}) copy-start(bf16[1,1024,1024]{1,2,0:T(8,128)(2,1)S(1)} %copy.180) | copy-start | bytes 6291460
  18.9 15.6 %copy-start.40 = (f32[1024]{0:T(1024)}, f32[1024]{0:T(1024)S(1)}, u32[]{:S(2)}) copy-start(f32[1024]{0:T(1024)S(1)} %fusion.91) | copy-start | bytes 12292
  19.0 290.2 %copy-start.36 = (f32[1024]{0:T(1024)}, f32[1024]{0:T(1024)S(1)}, u32[]{:S(2)}) copy-start(f32[1024]{0:T(1024)S(1)} %fusion.144) | copy-start | bytes 12292
  28.5 280.7 %copy-start.38 = (f32[4,1,256]{2,1,0:T(1,128)}, f32[4,1,256]{2,1,0:T(1,128)S(1)}, u32[]{:S(2)}) copy-start(f32[4,1,256]{2,1,0:T(1,128)S(1)} %convert_element_type.341) | copy-start | bytes 12292
  28.5 6.0 copy-start.48
  30.4 12.8 copy-start.49
  30.4 20.0 %copy-start.52 = (bf16[128]{0:T(256)(128)(2,1)S(1)}, bf16[128]{0:T(256)(128)(2,1)}, u32[]{:S(2)}) copy-start(bf16[128]{0:T(256)(128)(2,1)} %param.31) | copy-start | bytes 772
  42.6 19.1 %copy-start.32 = (bf16[1024,16]{0,1:T(8,128)(2,1)}, bf16[1024,16]{0,1:T(8,128)(2,1)S(1)}, u32[]{:S(2)}) copy-start(bf16[1024,16]{0,1:T(8,128)(2,1)S(1)} %all_gather.53) | copy-start | bytes 98308
  43.2 54.1 %copy-start.42 = (bf16[1024,16]{0,1:T(8,128)(2,1)}, bf16[1024,16]{0,1:T(8,128)(2,1)S(1)}, u32[]{:S(2)}) copy-start(bf16[1024,16]{0,1:T(8,128)(2,1)S(1)} %convolution_convert_fusion.5) | copy-start | bytes 98308
  50.4 7.8 copy-start.34
  58.2 6.4 copy-start.46
  58.2 6.9 copy-start.50
  58.2 7.6 copy-start.51
  58.2 8.8 copy-start.57
  58.2 18.5 %copy-start.58 = (bf16[256]{0:T(256)(128)(2,1)S(1)}, bf16[256]{0:T(256)(128)(2,1)}, u32[]{:S(2)}) copy-start(bf16[256]{0:T(256)(128)(2,1)} %param.34) | copy-start | bytes 1540
  92.7 4.6 copy-start.22
  92.7 4.6 copy-start.26
  293.6 7.1 copy-start
  338.1 44.1 %copy-start.19 = (bf16[1,1024,1024]{2,1,0:T(8,128)(2,1)S(1)}, bf16[1,1024,1024]{2,1,0:T(8,128)(2,1)}, u32[]{:S(2)}) copy-start(bf16[1,1024,1024]{2,1,0:T(8,128)(2,1)} %param.23) | copy-start | bytes 6291460
  403.8 10.2 copy-start.8
  403.8 10.2 copy-start.53
  403.8 10.2 copy-start.62
  414.0 6.5 copy-start.14
  420.6 4.3 copy-start.60
  420.6 5.5 copy-start.61
  421.6 10.5 copy-start.9
  432.2 5.7 copy-start.45
  437.9 4.6 copy-start.1
  437.9 5.9 copy-start.4
  714.3 89.4 %reduce-scatter.15.cloned.1.call-start = ((), (), s32[]{:S(2)}) async-start(), calls=%async_computation.19 | async-start | bytes 1310720 | tf_op jit(solution)/shard_map/reduce_scatter | solution.py:268
  719.7 7.4 copy-start.13
  719.7 92.0 %reduce-scatter.23.cloned.1.call-start = ((), (), s32[]{:S(2)}) async-start(), calls=%async_computation.23 | async-start | bytes 2621440 | tf_op jit(solution)/shard_map/reduce_scatter | solution.py:289
  726.6 124.0 %reduce-scatter.17.cloned.1.call-start = ((), (), s32[]{:S(2)}) async-start(), calls=%async_computation.20 | async-start | bytes 2621440 | tf_op jit(solution)/shard_map/reduce_scatter | solution.py:271
  730.7 3.8 copy-start.37
  730.7 3.8 copy-start.39
  734.4 154.4 %reduce-scatter.19.cloned.1.call-start = ((), (), s32[]{:S(2)}) async-start(), calls=%async_computation.21 | async-start | bytes 2621440 | tf_op jit(solution)/shard_map/reduce_scatter | solution.py:274
  739.8 217.9 %reduce-scatter.25.cloned.1.call-start = ((), (), s32[]{:S(2)}) async-start(), calls=%async_computation.24 | async-start | bytes 7208960 | tf_op jit(solution)/shard_map/reduce_scatter | solution.py:245
  750.8 275.8 %reduce-scatter.27.cloned.1.call-start = ((), (), s32[]{:S(2)}) async-start(), calls=%async_computation.25 | async-start | bytes 7208960 | tf_op jit(solution)/shard_map/reduce_scatter | solution.py:248
  762.0 333.6 %reduce-scatter.29.cloned.1.call-start = ((), (), s32[]{:S(2)}) async-start(), calls=%async_computation.26 | async-start | bytes 7208960 | tf_op jit(solution)/shard_map/reduce_scatter | solution.py:251
  773.3 4.3 copy-start.47
  773.4 365.9 %reduce-scatter.31.cloned.1.call-start = ((), (), s32[]{:S(2)}) async-start(), calls=%async_computation.27 | async-start | bytes 163840
  777.7 4.2 copy-start.35
  784.2 364.3 %reduce-scatter.21.cloned.1.call-start = ((), (), s32[]{:S(2)}) async-start(), calls=%async_computation.22 | async-start | bytes 40960 | tf_op jit(solution)/shard_map/reduce_scatter | solution.py:277
  785.6 507.3 %all-reduce.11.cloned.1.call-start = ((), (), s32[]{:S(2)}) async-start(), calls=%async_computation.28 | async-start | bytes 12845056 | tf_op jit(solution)/shard_map/psum | solution.py:295
  785.9 6.7 copy-start.18
  795.9 4.4 copy-start.16
  795.9 4.4 copy-start.17
  803.7 292.0 %copy-start.33 = (bf16[1024,16]{0,1:T(8,128)(2,1)S(1)}, bf16[1024,16]{0,1:T(8,128)(2,1)}, u32[]{:S(2)}) copy-start(bf16[1024,16]{0,1:T(8,128)(2,1)} %copy-done.32) | copy-start | bytes 98308
  1095.7 18.5 %copy-start.41 = (f32[1024]{0:T(1024)S(1)}, f32[1024]{0:T(1024)}, u32[]{:S(2)}) copy-start(f32[1024]{0:T(1024)} %copy-done.40) | copy-start | bytes 12292
  1293.0 5.1 copy-start.24
  1296.3 4.8 copy-start.28
  1298.0 4.1 copy-start.27
  1298.0 5.2 copy-start.31
  1298.0 6.1 copy-start.30
  (18 other events, 45.1 us)
Sparse Core Ops, SparseCore 0:
  9.9 29.3 all-gather.11
  41.1 26.8 all-gather.15
  69.9 35.3 all-gather.13
  106.9 35.2 all-gather.17
  144.0 35.2 all-gather.19
  181.0 65.7 all-gather.21
  248.7 65.7 all-gather.23
  316.4 65.7 all-gather.25
  714.4 27.7 reduce-scatter.12
  745.7 27.7 reduce-scatter.14
  776.5 35.1 reduce-scatter.22
  815.4 35.1 reduce-scatter.16
  853.5 35.1 reduce-scatter.18
  891.9 65.8 reduce-scatter.24
  960.9 65.7 reduce-scatter.26
  1029.8 65.7 reduce-scatter.28
  1099.0 23.8 reduce-scatter.30
  1126.0 22.4 reduce-scatter.20
  1151.5 141.4 all-reduce.10
where the time goes:
time: 1320 us; the launch traced here: 1310 us
  waiting for transfers between devices  454 us (34%)
  matrix products  359 us (27%)
  local copies, waits for them, and re-layouts  218 us (17%)
  other arithmetic  130 us (10%)
  blocking collectives  87.2 us (7%)
  loops' own time  44.2 us (3%)
  between operations  17.6 us (1%)
    psum x1, waiting for transfers between devices, local(): lax.psum(mixer_rows[1].astype(jnp.bfloat16), 'rep').astype(jnp.float32)  112 us
    dot_general x10, matrix products, right_trans(): lax.dot_general(left, right, (((1,), (1,)), ((), ())), preferred_element_...  73.3 us
    reduce_scatter x1, waiting for transfers between devices, local(): lax.psum_scatter(part_gate.astype(jnp.bfloat16), 'shard', scatter_dimensi...  69 us
    reduce_scatter x1, waiting for transfers between devices, local(): lax.psum_scatter(part_down.astype(jnp.bfloat16), 'shard', scatter_dimensi...  68.9 us
    reduce_scatter x1, waiting for transfers between devices, local(): lax.psum_scatter(part_up.astype(jnp.bfloat16), 'shard', scatter_dimension...  68.9 us
    dot_general x10, matrix products, matmul(): return jnp.dot(left, right, preferred_element_type=jnp.float32)  66.2 us
    squeeze x96, local copies, waits for them, and re-layouts, block_pass(): lax.scan(jax.checkpoint(advance), start, (shaped(query), shaped(keys), sh...  61.5 us
    dynamic_slice x80, local copies, waits for them, and re-layouts, block_pass(): lax.scan(jax.checkpoint(advance), start, (shaped(query), shaped(keys), sh...  59.3 us
  transfers between devices with their start and end apart: 19, of which 10 were waited for; matrix products, arithmetic and copies ran while one was open for 29% of the time, Pallas kernels for 0%

commit v1 on v0

--- a/solution.py
+++ b/solution.py
@@ -10,6 +10,25 @@
 BLOCK = 64
 VD = 1024
 HEAD_EPS = 1.0
+
+
+def collect(x, axis, dim):
+    size, index, rows = (lax.axis_size(axis), lax.axis_index(axis), x.shape[dim])
+    right = [(i, (i + 1) % size) for i in range(size)]
+    left = [(i, (i - 1) % size) for i in range(size)]
+    out = jnp.zeros((*x.shape[:dim], size * rows, *x.shape[dim + 1 :]), x.dtype)
+    out = lax.dynamic_update_slice_in_dim(out, x, index * rows, axis=dim)
+    from_left = from_right = x
+    half = size // 2
+    for hop in range(1, half + 1):
+        from_left = lax.ppermute(from_left, axis, right)
+        out = lax.dynamic_update_slice_in_dim(out, from_left, (index - hop) % size * rows, axis=dim)
+        if hop < size - half:
+            from_right = lax.ppermute(from_right, axis, left)
+            out = lax.dynamic_update_slice_in_dim(
+                out, from_right, (index + hop) % size * rows, axis=dim
+            )
+    return out
 
 
 def matmul(left, right):
@@ -130,7 +149,7 @@
         lax.all_gather(norm_mlp, "shard", axis=0, tiled=True),
         lax.all_gather(w_gate, "shard", axis=0, tiled=True),
         lax.all_gather(w_up, "shard", axis=0, tiled=True),
-        lax.all_gather(w_down, "shard", axis=0, tiled=True),
+        collect(w_down, "shard", 0),
     )
     gain_mix, query_w, key_w, value_w, outgate_w, low_w, high_w, bias_w, headgain_w, out_w = (
         mixer_full

time: 1320 us -> 1360 us (1.030)
  waiting for transfers between devices: 454 us -> 487 us
    ppermute x0 -> x3, waiting for transfers between devices: none -> 127 us  [the longest x2 88.6 us: collect(): from_left = lax.ppermute(from_left, axis, right)]
    reduce_scatter x1, waiting for transfers between devices: 38.9 us -> 0.02 us  [local(): lax.psum_scatter(part_value.astype(jnp.bfloat16), 'shard', scatter_dimens...]
    reduce_scatter x1, waiting for transfers between devices: 38.2 us -> 0.02 us  [local(): lax.psum_scatter(part_outgate.astype(jnp.bfloat16), 'shard', scatter_dime...]
    unnamed x147 -> x159, local copies, waits for them, and re-layouts: 38.4 us -> 40.6 us
  transfers between devices with their start and end apart: 19 -> 22, of which waited for: 10 -> 10; matrix products, arithmetic and copies ran while one was open for 29% -> 28% of each run, Pallas kernels for 0% -> 0%
where the time goes in v1:
time: 1360 us; the launch traced here: 1350 us
  waiting for transfers between devices  487 us (36%)
  matrix products  358 us (26%)
  local copies, waits for them, and re-layouts  225 us (17%)
  other arithmetic  128 us (9%)
  blocking collectives  87.2 us (6%)
  loops' own time  44.2 us (3%)
  between operations  17.7 us (1%)
    psum x1, waiting for transfers between devices, local(): lax.psum(mixer_rows[1].astype(jnp.bfloat16), 'rep').astype(jnp.float32)  112 us
    ppermute x2, waiting for transfers between devices, collect(): from_left = lax.ppermute(from_left, axis, right)  88.6 us
    dot_general x10, matrix products, right_trans(): lax.dot_general(left, right, (((1,), (1,)), ((), ())), preferred_element_...  72.8 us
    reduce_scatter x1, waiting for transfers between devices, local(): lax.psum_scatter(part_down.astype(jnp.bfloat16), 'shard', scatter_dimensi...  68.9 us
    reduce_scatter x1, waiting for transfers between devices, local(): lax.psum_scatter(part_up.astype(jnp.bfloat16), 'shard', scatter_dimension...  68.9 us
    dot_general x10, matrix products, matmul(): return jnp.dot(left, right, preferred_element_type=jnp.float32)  66.5 us
    squeeze x96, local copies, waits for them, and re-layouts, block_pass(): lax.scan(jax.checkpoint(advance), start, (shaped(query), shaped(keys), sh...  61.6 us
    reduce_scatter x1, waiting for transfers between devices, local(): lax.psum_scatter(part_gate.astype(jnp.bfloat16), 'shard', scatter_dimensi...  59.7 us
  transfers between devices with their start and end apart: 22, of which 10 were waited for; matrix products, arithmetic and copies ran while one was open for 28% of the time, Pallas kernels for 0%

profile of v1, /device:TPU:0, one launch (start us, length us, event | category | flops | bytes accessed | tf_op | source)
XLA Modules:
  0.0 1352.5 jit_solution(10711363654295205862)
XLA Ops:
  15.5 2.9 copy.180
  18.9 9.5 all-gather
  30.3 4.1 copy.181
  34.5 8.0 all_gather.52
  43.1 7.2 all_gather.53
  50.4 7.7 all-gather.1
  58.2 3.4 negate_multiply_fusion
  61.6 2.9 reshape.789
  67.2 8.9 all-reduce.1
  76.7 7.2 all-gather.2
  84.0 4.1 copy.194
  88.1 2.3 copy.182
  90.3 2.3 copy.184
  92.6 4.6 fusion.120
  97.2 2.6 fusion.158
  99.8 5.5 all-gather.14.cloned.1.call-done
  105.3 3.9 copy.183
  109.2 6.5 convolution_bitcast_fusion.6
  115.8 177.9 %while.44 = (s32[]{:T(128)}, f32[1,4,128,256]{3,2,1,0:T(8,128)S(1)}, s32[1]{0:T(128)}, f32[16,1,64,4,256]{4,2,3,1,0:T(8,128)}, f32[16,1,4,128,256]{4,3,2,1,0:T(8...) while((s32[]{:T(128)}, ...), condition=%wide.region_3.4_spmd.clone.clone, body=%wide.region_1.3_spmd.clone.sunk.clone | while | flops 280002816 | bytes 6207163 | solution.py:93
  293.7 7.1 copy.190
  303.2 3.0 copy.250
  306.2 3.0 copy.249
  309.2 8.6 multiply_convert_fusion.4
  317.8 4.8 multiply_reduce_fusion.6
  326.5 11.6 fusion.159
  338.1 12.9 fusion.160
  351.0 31.3 %all-gather.26.cloned.1.call-done = bf16[2816,1024]{1,0:T(8,128)(2,1)} async-done(((bf16[704,1024]{1,0:T(8,128)(2,1)}), bf16[2816,1024]{1,0:T(8,128)(2,1)}) %all-gather.26.cloned.1.call-update) | async-done | bytes 5767184 | tf_op jit(solution)/shard_map/all_gather | solution.py:194
  382.3 21.4 %multiply_convert_fusion = (bf16[1024,2816]{1,0:T(8,128)(2,1)}, bf16[1024,2816]{1,0:T(8,128)(2,1)}, bf16[1024,2816]{1,0:T(8,128)(2,1)}) fusion(f32[1024,2816]{1,0:T(8,128)} %fusion.159, f32[1024,2816]{1,0:T(8,128)} %fusion.160, bf16[2816,1024]{1,0:T(8,128)(2,1)} %all-gather.26.cloned.1.call-done, bf16[1,1024,1024]{2,1,0:T(8,128)(2,1)S(1)} %copy-done.25), kind=kOutput, calls=%fused_computation.120 | convolution fusion | flops 5948833792 | bytes 48234496 | tf_op jit(solution)/shard_map/dot_general | solution.py:45
  403.8 10.2 fusion.161
  414.0 6.5 multiply_reduce_fusion.2
  422.2 2.7 copy-done.66
  426.1 6.0 multiply_reduce_fusion.3
  432.1 5.6 reshape.794
  437.8 4.4 multiply_reduce_fusion.4
  443.7 2.6 add_add_fusion.1
  449.7 258.5 %while.45 = (s32[]{:T(128)}, f32[1,4,128,256]{2,3,1,0:T(8,128)S(1)}, f32[16,1,64,4,128]{4,2,3,1,0:T(8,128)}, bf16[16,1,64,4,128]{4,2,3,1,0:T(8,128)(2,1)S(1)}, b...) while((s32[]{:T(128)}, ...), condition=%wide.region_13.14_spmd.clone.clone, body=%wide.region_8.13_spmd.clone.sunk.clone | while | flops 585089280 | bytes 16077553 | solution.py:93
  712.2 2.2 fusion.123
  716.3 2.3 fusion.126
  718.7 6.8 convolution_convert_fusion.3
  729.6 3.7 fusion.117
  733.4 5.3 convolution_convert_fusion.4
  738.8 10.9 convolution_convert_fusion.2
  749.7 11.1 convolution_convert_fusion.1
  761.0 11.2 convolution_convert_fusion
  776.5 47.3 %collective-permute-done = bf16[704,1024]{1,0:T(8,128)(2,1)} collective-permute-done((bf16[704,1024]{1,0:T(8,128)(2,1)S(1)}, bf16[704,1024]{1,0:T(8,128)(2,1)}, u32[]{:S(2)}, u32[]{:S(2)}) %collective-permute-start) | collective-permute-done | bytes 1441824 | tf_op jit(solution)/shard_map/ppermute | solution.py:24
  829.7 38.2 %collective-permute-done.1 = bf16[704,1024]{1,0:T(8,128)(2,1)} collective-permute-done((bf16[704,1024]{1,0:T(8,128)(2,1)S(1)}, bf16[704,1024]{1,0:T(8,128)(2,1)}, u32[]{:S(2)}, u32[]{:S(2)}) %collective-permute-start.1) | collective-permute-done | bytes 1441824 | tf_op jit(solution)/shard_map/ppermute | solution.py:27
  869.5 41.4 %collective-permute-done.2 = bf16[704,1024]{1,0:T(8,128)(2,1)} collective-permute-done((bf16[704,1024]{1,0:T(8,128)(2,1)}, bf16[704,1024]{1,0:T(8,128)(2,1)}, u32[]{:S(2)}, u32[]{:S(2)}) %collective-permute-start.2) | collective-permute-done | bytes 1441824 | tf_op jit(solution)/shard_map/ppermute | solution.py:24
  920.9 6.8 fusion.162
  927.7 3.3 fusion.133
  931.1 4.4 fusion.163
  935.5 3.3 fusion.130
  938.8 59.7 %reduce-scatter.25.cloned.1.call-done = bf16[256,2816]{1,0:T(8,128)(2,1)} async-done(((bf16[1024,2816]{1,0:T(8,128)(2,1)}), bf16[256,2816]{1,0:T(8,128)(2,1)}) %reduce-scatter.25.cloned.1.call-update) | async-done | bytes 1441808 | tf_op jit(solution)/shard_map/reduce_scatter | solution.py:264
  998.5 68.9 %reduce-scatter.27.cloned.1.call-done = bf16[256,2816]{1,0:T(8,128)(2,1)} async-done(((bf16[1024,2816]{1,0:T(8,128)(2,1)}), bf16[256,2816]{1,0:T(8,128)(2,1)}) %reduce-scatter.27.cloned.1.call-update) | async-done | bytes 1441808 | tf_op jit(solution)/shard_map/reduce_scatter | solution.py:267
  1067.4 68.9 %reduce-scatter.29.cloned.1.call-done = bf16[704,1024]{1,0:T(8,128)(2,1)} async-done(((bf16[2816,1024]{1,0:T(8,128)(2,1)}), bf16[704,1024]{1,0:T(8,128)(2,1)}) %reduce-scatter.29.cloned.1.call-update) | async-done | bytes 1441808 | tf_op jit(solution)/shard_map/reduce_scatter | solution.py:270
  1136.4 8.9 fusion.90
  1145.4 9.4 all-reduce.8
  1154.9 6.5 fusion.100
  1161.4 5.4 copy.213
  1166.7 10.8 fusion.102
  1177.5 2.6 copy.212
  1181.1 8.2 reduce-scatter.21.cloned.1.call-done
  1189.2 29.1 %all-reduce.6 = (bf16[256]{0:T(256)(128)(2,1)S(1)}, bf16[256,16]{0,1:T(8,128)(2,1)S(1)}, bf16[16,128]{1,0:T(8,128)(2,1)S(1)}, bf16[128]{0:T(256)(128)(2,1)S(1)},...) all-reduce(bf16[256]{0:T(256)(128)(2,1)S(1)} %dynamic-slice.2, ...), channel_id=1, replica_groups=mesh['rep'=8,'shard'=4] {'rep'}, use_global_device_ids=true, to_apply=%region_17.18 | all-reduce | flops 6848 | bytes 27392 | tf_op jit(solution)/shard_map/psum | solution.py:313
  1221.7 112.0 %all-reduce.11.cloned.1.call-done = (bf16[256,512]{1,0:T(8,128)(2,1)}, bf16[256,512]{1,0:T(8,128)(2,1)}, bf16[256,1024]{1,0:T(8,128)(2,1)}, bf16[256,1024]{1,0:T...) async-done(((bf16[256,512]{1,0:T(8,128)(2,1)}, bf16[256,512]{1,0:T(8,128)(2,1)}, ...) | async-done | bytes 6422544 | tf_op jit(solution)/shard_map/psum | solution.py:314
  1333.7 3.3 convert_element_type.335
  (984 shorter events, 463.3 us)
Async XLA Ops:
  7.2 80.9 %all-gather.12.cloned.1.call-start = ((), (), s32[]{:S(2)}) async-start(), calls=%async_computation.10 | async-start | bytes 1310720 | tf_op jit(solution)/shard_map/all_gather | solution.py:139
  7.9 82.4 %all-gather.16.cloned.1.call-start = ((), (), s32[]{:S(2)}) async-start(), calls=%async_computation.12 | async-start | bytes 1310720 | tf_op jit(solution)/shard_map/all_gather | solution.py:138
  8.7 96.6 %all-gather.14.cloned.1.call-start = ((), (), s32[]{:S(2)}) async-start(), calls=%async_computation.11 | async-start | bytes 2621440 | tf_op jit(solution)/shard_map/all_gather | solution.py:140
  9.4 299.8 %all-gather.18.cloned.1.call-start = ((), (), s32[]{:S(2)}) async-start(), calls=%async_computation.13 | async-start | bytes 2621440 | tf_op jit(solution)/shard_map/all_gather | solution.py:141
  10.0 307.9 %all-gather.20.cloned.1.call-start = ((), (), s32[]{:S(2)}) async-start(), calls=%async_computation.14 | async-start | bytes 2621440 | tf_op jit(solution)/shard_map/all_gather | solution.py:146
  10.6 314.6 %all-gather.22.cloned.1.call-start = ((), (), s32[]{:S(2)}) async-start(), calls=%async_computation.15 | async-start | bytes 7208960 | tf_op jit(solution)/shard_map/all_gather | solution.py:150
  11.1 327.0 %all-gather.24.cloned.1.call-start = ((), (), s32[]{:S(2)}) async-start(), calls=%async_computation.16 | async-start | bytes 7208960 | tf_op jit(solution)/shard_map/all_gather | solution.py:151
  11.9 370.4 %all-gather.26.cloned.1.call-start = ((), (), s32[]{:S(2)}) async-start(), calls=%async_computation.17 | async-start | bytes 7208960 | tf_op jit(solution)/shard_map/all_gather | solution.py:194
  12.6 926.1 %reduce-scatter.13.cloned.1.call-start = ((), (), s32[]{:S(2)}) async-start(), calls=%async_computation.18 | async-start | bytes 1310720 | tf_op jit(solution)/shard_map/reduce_scatter | solution.py:284
  14.3 4.6 copy-start.62
  18.4 299.4 %copy-start.2 = (bf16[1,1024,1024]{1,2,0:T(8,128)(2,1)}, bf16[1,1024,1024]{1,2,0:T(8,128)(2,1)S(1)}, u32[]{:S(2)}) copy-start(bf16[1,1024,1024]{1,2,0:T(8,128)(2,1)S(1)} %copy.180) | copy-start | bytes 6291460
  18.9 15.6 %copy-start.46 = (f32[1024]{0:T(1024)}, f32[1024]{0:T(1024)S(1)}, u32[]{:S(2)}) copy-start(f32[1024]{0:T(1024)S(1)} %fusion.91) | copy-start | bytes 12292
  18.9 290.3 %copy-start.42 = (f32[1024]{0:T(1024)}, f32[1024]{0:T(1024)S(1)}, u32[]{:S(2)}) copy-start(f32[1024]{0:T(1024)S(1)} %fusion.144) | copy-start | bytes 12292
  28.5 280.7 %copy-start.44 = (f32[4,1,256]{2,1,0:T(1,128)}, f32[4,1,256]{2,1,0:T(1,128)S(1)}, u32[]{:S(2)}) copy-start(f32[4,1,256]{2,1,0:T(1,128)S(1)} %convert_element_type.341) | copy-start | bytes 12292
  28.5 6.0 copy-start.54
  30.3 12.8 copy-start.55
  30.3 20.0 %copy-start.58 = (bf16[128]{0:T(256)(128)(2,1)S(1)}, bf16[128]{0:T(256)(128)(2,1)}, u32[]{:S(2)}) copy-start(bf16[128]{0:T(256)(128)(2,1)} %param.31) | copy-start | bytes 772
  42.5 19.1 %copy-start.38 = (bf16[1024,16]{0,1:T(8,128)(2,1)}, bf16[1024,16]{0,1:T(8,128)(2,1)S(1)}, u32[]{:S(2)}) copy-start(bf16[1024,16]{0,1:T(8,128)(2,1)S(1)} %all_gather.52) | copy-start | bytes 98308
  43.1 54.1 %copy-start.48 = (bf16[1024,16]{0,1:T(8,128)(2,1)}, bf16[1024,16]{0,1:T(8,128)(2,1)S(1)}, u32[]{:S(2)}) copy-start(bf16[1024,16]{0,1:T(8,128)(2,1)S(1)} %convolution_convert_fusion.5) | copy-start | bytes 98308
  50.4 7.8 copy-start.40
  58.1 6.4 copy-start.52
  58.1 6.9 copy-start.56
  58.1 7.6 copy-start.57
  58.1 8.8 copy-start.63
  58.2 18.5 %copy-start.64 = (bf16[256]{0:T(256)(128)(2,1)S(1)}, bf16[256]{0:T(256)(128)(2,1)}, u32[]{:S(2)}) copy-start(bf16[256]{0:T(256)(128)(2,1)} %param.34) | copy-start | bytes 1540
  92.6 4.6 copy-start.28
  92.6 4.6 copy-start.32
  293.7 7.1 copy-start
  338.1 44.2 %copy-start.25 = (bf16[1,1024,1024]{2,1,0:T(8,128)(2,1)S(1)}, bf16[1,1024,1024]{2,1,0:T(8,128)(2,1)}, u32[]{:S(2)}) copy-start(bf16[1,1024,1024]{2,1,0:T(8,128)(2,1)} %param.23) | copy-start | bytes 6291460
  403.8 10.2 copy-start.8
  403.8 10.2 copy-start.59
  403.8 10.2 copy-start.68
  414.0 6.5 copy-start.15
  420.6 5.5 copy-start.67
  421.6 10.5 copy-start.9
  432.1 5.6 copy-start.51
  437.7 4.6 copy-start.1
  437.7 5.9 copy-start.4
  714.4 224.4 %reduce-scatter.15.cloned.1.call-start = ((), (), s32[]{:S(2)}) async-start(), calls=%async_computation.19 | async-start | bytes 1310720 | tf_op jit(solution)/shard_map/reduce_scatter | solution.py:287
  718.6 7.3 copy-start.13
  718.6 220.1 %reduce-scatter.23.cloned.1.call-start = ((), (), s32[]{:S(2)}) async-start(), calls=%async_computation.23 | async-start | bytes 2621440 | tf_op jit(solution)/shard_map/reduce_scatter | solution.py:308
  725.5 213.3 %reduce-scatter.17.cloned.1.call-start = ((), (), s32[]{:S(2)}) async-start(), calls=%async_computation.20 | async-start | bytes 2621440 | tf_op jit(solution)/shard_map/reduce_scatter | solution.py:290
  733.3 205.5 %reduce-scatter.19.cloned.1.call-start = ((), (), s32[]{:S(2)}) async-start(), calls=%async_computation.21 | async-start | bytes 2621440 | tf_op jit(solution)/shard_map/reduce_scatter | solution.py:293
  738.7 259.8 %reduce-scatter.25.cloned.1.call-start = ((), (), s32[]{:S(2)}) async-start(), calls=%async_computation.24 | async-start | bytes 7208960 | tf_op jit(solution)/shard_map/reduce_scatter | solution.py:264
  749.7 317.7 %reduce-scatter.27.cloned.1.call-start = ((), (), s32[]{:S(2)}) async-start(), calls=%async_computation.25 | async-start | bytes 7208960 | tf_op jit(solution)/shard_map/reduce_scatter | solution.py:267
  760.8 375.5 %reduce-scatter.29.cloned.1.call-start = ((), (), s32[]{:S(2)}) async-start(), calls=%async_computation.26 | async-start | bytes 7208960 | tf_op jit(solution)/shard_map/reduce_scatter | solution.py:270
  772.2 408.0 %reduce-scatter.31.cloned.1.call-start = ((), (), s32[]{:S(2)}) async-start(), calls=%async_computation.27 | async-start | bytes 163840
  773.6 50.2 %collective-permute-start = (bf16[704,1024]{1,0:T(8,128)(2,1)S(1)}, bf16[704,1024]{1,0:T(8,128)(2,1)}, u32[]{:S(2)}, u32[]{:S(2)}) collective-permute-start(bf16[704,1024]{1,0:T(8,128)(2,1)S(1)} %copy-done.17), channel_id=1, source_target_pairs={{0,1},{1,2},{2,3},{3,0},{4,5},{5,6},{6,7},{7,4},{8,9},{9,10},{10,1... | collective-permute-start | bytes 4325384 | tf_op jit(solution)/shard_map/ppermute | solution.py:24
  774.9 93.0 %collective-permute-start.1 = (bf16[704,1024]{1,0:T(8,128)(2,1)S(1)}, bf16[704,1024]{1,0:T(8,128)(2,1)}, u32[]{:S(2)}, u32[]{:S(2)}) collective-permute-start(bf16[704,1024]{1,0:T(8,128)(2,1)S(1)} %copy-done.17), channel_id=1, source_target_pairs={{0,3},{1,0},{2,1},{3,2},{4,7},{5,4},{6,5},{7,6},{8,11},{9,8},{10,9... | collective-permute-start | bytes 4325384 | tf_op jit(solution)/shard_map/ppermute | solution.py:27
  823.8 87.0 %collective-permute-start.2 = (bf16[704,1024]{1,0:T(8,128)(2,1)}, bf16[704,1024]{1,0:T(8,128)(2,1)}, u32[]{:S(2)}, u32[]{:S(2)}) collective-permute-start(bf16[704,1024]{1,0:T(8,128)(2,1)} %collective-permute-done), channel_id=1, source_target_pairs={{0,1},{1,2},{2,3},{3,0},{4,5},{5,6},{6,7},{7,4},{8,9},{9,10},{10,1... | collective-permute-start | bytes 4325384 | tf_op jit(solution)/shard_map/ppermute | solution.py:24
  828.0 84.3 %copy-start.14 = (f32[16,1,64,4,128]{4,3,2,1,0:T(4,128)S(1)}, f32[16,1,64,4,128]{4,3,2,1,0:T(4,128)}, u32[]{:S(2)}) copy-start(f32[16,1,64,4,128]{4,3,2,1,0:T(4,128)} %get-tuple-element.392) | copy-start | bytes 6291460
  869.4 43.5 %copy-start.29 = (f32[1024,512]{1,0:T(8,128)S(1)}, f32[1024,512]{1,0:T(8,128)}, u32[]{:S(2)}) copy-start(f32[1024,512]{1,0:T(8,128)} %get-tuple-element.753) | copy-start | bytes 6291460
  869.5 43.5 %copy-start.53 = (f32[4,1,128]{2,1,0:T(1,128)S(1)}, f32[4,1,128]{2,1,0:T(1,128)}, u32[]{:S(2)}) copy-start(f32[4,1,128]{2,1,0:T(1,128)} %copy-done.52) | copy-start | bytes 6148
  919.2 270.0 %reduce-scatter.21.cloned.1.call-start = ((), (), s32[]{:S(2)}) async-start(), calls=%async_computation.22 | async-start | bytes 40960 | tf_op jit(solution)/shard_map/reduce_scatter | solution.py:296
  920.6 7.1 copy-start.19
  920.7 413.1 %all-reduce.11.cloned.1.call-start = ((), (), s32[]{:S(2)}) async-start(), calls=%async_computation.28 | async-start | bytes 12845056 | tf_op jit(solution)/shard_map/psum | solution.py:314
  920.9 6.8 copy-start.24
  931.1 4.4 copy-start.23
  938.8 197.6 %copy-start.39 = (bf16[1024,16]{0,1:T(8,128)(2,1)S(1)}, bf16[1024,16]{0,1:T(8,128)(2,1)}, u32[]{:S(2)}) copy-start(bf16[1024,16]{0,1:T(8,128)(2,1)} %copy-done.38) | copy-start | bytes 98308
  1136.4 18.5 %copy-start.47 = (f32[1024]{0:T(1024)S(1)}, f32[1024]{0:T(1024)}, u32[]{:S(2)}) copy-start(f32[1024]{0:T(1024)} %copy-done.46) | copy-start | bytes 12292
  1333.7 5.1 copy-start.30
  1337.0 4.8 copy-start.34
  1338.8 5.2 copy-start.37
  1338.8 6.1 copy-start.36
  (27 other events, 76.7 us)
Sparse Core Ops, SparseCore 0:
  9.9 29.4 all-gather.11
  41.2 26.8 all-gather.15
  69.9 35.3 all-gather.13
  107.0 35.2 all-gather.17
  144.0 35.2 all-gather.19
  181.1 65.8 all-gather.21
  248.8 65.7 all-gather.23
  316.5 65.7 all-gather.25
  714.5 27.6 reduce-scatter.12
  745.2 27.7 reduce-scatter.14
  776.0 52.1 reduce-scatter.22
  831.9 53.1 reduce-scatter.16
  888.1 41.3 reduce-scatter.18
  932.6 65.8 reduce-scatter.24
  1001.6 65.7 reduce-scatter.26
  1070.5 65.7 reduce-scatter.28
  1139.7 23.8 reduce-scatter.30
  1166.8 22.4 reduce-scatter.20
  1192.2 141.4 all-reduce.10
